TPU v7x, 512 devices: a whole 4x4x16 slice. The times are simulated.
512 devices in a mesh: prow: 32 (over y, x, core), pcol: 16 (over z).
Axes of the slice: x: 4, y: 4, z: 16, core: 2. Of those that a mesh axis runs over, the one named last changes fastest.
Arguments:
- inverse_blocks: bfloat16 [128, 128, 128, 128], P('pcol', 'prow'), may hold values from -6 to 6
- lower_blocks: bfloat16 [128, 4, 128, 128], P('prow', None, 'pcol'), may hold values from -0.625 to 0.625
- pattern: int32 [4, 64], replicated, may hold values from 0 to 127, as said below
- diag_inverse: float32 [4, 16384], P(None, ('prow', 'pcol')), may hold values from -6 to 6
Outputs:
- inverse_column: float32 [128, 4, 128, 128], P('pcol', None, 'prow')
- inverse_diag: float32 [4, 16384], P(None, ('prow', 'pcol'))
Inputs may be any that keep to these rules, and one draw needn't show every extreme that they name: `pattern`: each row names 64 different ancestor blocks.
All inputs are finite; a program needn't handle non-finite values.
Results may differ from a plain program's by a relative error of at most 0.0003.
Values may be sent and summed in bfloat16 or wider, within the bound.
A program may use at most 64 MiB of HBM per device.

v0:
```python
import jax
import jax.numpy as jnp
from jax import lax
from jax.sharding import PartitionSpec as P


def broadcast(x, axis, root):
    mine = lax.axis_index(axis) == root
    return lax.psum(jnp.where(mine, x, jnp.zeros_like(x)), axis)


def per_device(inverse_blocks, lower_blocks, pattern, diag_inverse):
    blocks_i = inverse_blocks.shape[0]
    blocks_j = inverse_blocks.shape[1]
    block_width = inverse_blocks.shape[3]
    node_count = lower_blocks.shape[1]
    row_groups = lax.axis_size("prow")
    col_groups = lax.axis_size("pcol")
    block_count = blocks_j * row_groups
    ratio = row_groups // col_groups
    row_share = block_width // row_groups
    matches = pattern[None, :, :] == jnp.arange(block_count, dtype=jnp.int32)[:, None, None]
    present = jnp.sum(matches.astype(jnp.float32), axis=2)
    start_j = lax.axis_index("prow") * blocks_j
    start_i = lax.axis_index("pcol") * blocks_i
    keep_j = lax.dynamic_slice_in_dim(present, start_j, blocks_j, 0)
    keep_i = lax.dynamic_slice_in_dim(present, start_i, blocks_i, 0)
    whole = lax.all_gather(lower_blocks, "pcol", axis=2, tiled=True)
    masked = whole * keep_j.astype(jnp.bfloat16)[:, :, None, None]
    summed = lax.psum_scatter(
        jnp.einsum("ijrb,jkbe->rike", inverse_blocks, masked, preferred_element_type=jnp.float32),
        "prow",
        scatter_dimension=0,
        tiled=True,
    )
    column = summed * (-keep_i)[None, :, :, None]
    row_begin = lax.axis_index("prow") * row_share
    pieces = []
    for offset in range(ratio):
        received = broadcast(masked, "prow", lax.axis_index("pcol") * ratio + offset)
        pieces.append(lax.dynamic_slice_in_dim(received, row_begin, row_share, 2))
    own_lower = jnp.concatenate(pieces, axis=0)
    partial_value = jnp.einsum(
        "ikra,rikb->kab", own_lower.astype(jnp.float32), column, precision=lax.Precision.HIGHEST
    )
    partial_value = partial_value.reshape(node_count, block_width * block_width)
    totals = lax.psum(partial_value, ("prow", "pcol"))
    piece_len = block_width * block_width // (row_groups * col_groups)
    flat_index = lax.axis_index("prow") * col_groups + lax.axis_index("pcol")
    diag_piece = lax.dynamic_slice_in_dim(totals, flat_index * piece_len, piece_len, 1)
    return (jnp.transpose(column, (1, 2, 0, 3)), diag_inverse - diag_piece)


def solution(mesh):
    placed = (
        P("pcol", "prow", None, None),
        P("prow", None, "pcol", None),
        P(),
        P(None, ("prow", "pcol")),
    )
    return jax.shard_map(
        per_device,
        mesh=mesh,
        in_specs=placed,
        out_specs=(P("pcol", None, "prow", None), P(None, ("prow", "pcol"))),
        check_vma=False,
    )
```

profile of v0, /device:TPU:4, one launch (start us, length us, event | category | flops | bytes accessed | tf_op | source)
XLA Modules:
  0.0 766.1 jit_solution(11507525416745244874)
XLA Ops:
  7.2 0.0 copy-start
  7.2 0.0 all-reduce.6.cloned.1.call-start
  7.2 0.9 convert_reduce_fusion
  8.1 0.8 copy.15
  8.9 38.5 %all_gather.3 = bf16[4,4,128,128]{3,0,2,1:T(4,128)(2,1)S(1)} all-gather(bf16[4,4,8,128]{3,0,2,1:T(4,128)(2,1)S(1)} %copy.15), channel_id=1, replica_groups=mesh['prow'=32,'pcol'=16] {'pcol'}, dimensions={2}, use_global_device_ids=true | all-gather | bytes 557056 | tf_op jit(solution)/shard_map/all_gather | solution.py:28
  47.4 0.1 dynamic-slice_convert_fusion
  47.5 1.6 broadcast_select_fusion.1
  49.1 0.0 all-reduce.6.cloned.1.call-update
  49.2 0.0 reduce-scatter.2.cloned.1.call-start
  49.2 0.0 copy-done
  49.2 1.8 convolution_bitcast_fusion
  51.0 2.0 copy.17
  53.1 0.0 copy-start.1
  53.1 0.0 reduce-scatter.2.cloned.1.call-update
  53.1 0.0 all-reduce.4.cloned.1.call-start
  53.2 0.1 dynamic-slice_negate_fusion
  53.2 127.3 %all-reduce.6.cloned.1.call-done = (bf16[4,4,128,128]{3,0,2,1:T(4,128)(2,1)}, bf16[4,4,128,128]{3,0,2,1:T(4,128)(2,1)}) async-done(((bf16[4,4,128,128]{3,0,2,1:T(4,128)(2,1)}, bf16[4,4,128,128]{3,0,2,1:T(4,128)(2,1)}), (bf16[4,4,128,128]{3,0,2,1:T(4,128)(2,1)}, bf16[4,4,128,128]{3,0,2,1:T(4,128)(2,1)})) %all-reduce.6.cloned.1.call-update) | async-done | bytes 1048592 | tf_op jit(solution)/shard_map/psum | solution.py:9
  180.5 0.7 constant_dynamic-slice_fusion
  181.2 105.8 %reduce-scatter.2.cloned.1.call-done = f32[4,8,4,128]{3,1,2,0:T(8,128)} async-done(((f32[128,8,4,128]{3,1,2,0:T(8,128)}), f32[4,8,4,128]{3,1,2,0:T(8,128)}) %reduce-scatter.2.cloned.1.call-update) | async-done | bytes 65552 | tf_op jit(solution)/shard_map/reduce_scatter | solution.py:30
  287.1 1.2 convolution_bitcast_fusion.1
  288.2 0.9 copy.31
  289.1 0.0 all-reduce.4.cloned.1.call-update
  289.1 0.9 fusion.7
  290.0 0.7 copy.19
  290.7 467.6 %all-reduce.4.cloned.1.call-done = f32[4,16384]{1,0:T(4,128)} async-done(((f32[4,16384]{1,0:T(4,128)}), f32[4,16384]{1,0:T(4,128)}) %all-reduce.4.cloned.1.call-update) | async-done | bytes 262160 | tf_op jit(solution)/shard_map/psum | solution.py:47
  758.3 0.0 copy-done.1
  758.3 1.3 dynamic-slice_subtract_fusion
Async XLA Ops:
  7.2 42.1 %copy-start = (bf16[8,4,128,128]{3,2,1,0:T(8,128)(2,1)S(1)}, bf16[8,4,128,128]{3,2,1,0:T(8,128)(2,1)}, u32[]{:S(2)}) copy-start(bf16[8,4,128,128]{3,2,1,0:T(8,128)(2,1)} %param.4) | copy-start | bytes 3145732
  7.2 173.3 %all-reduce.6.cloned.1.call-start = ((), (), s32[]{:S(2)}) async-start(), calls=%async_computation.3 | async-start | bytes 2097152 | tf_op jit(solution)/shard_map/psum | solution.py:9
  49.2 237.9 %reduce-scatter.2.cloned.1.call-start = ((), (), s32[]{:S(2)}) async-start(), calls=%async_computation.1 | async-start | bytes 2162688 | tf_op jit(solution)/shard_map/reduce_scatter | solution.py:30
  53.1 705.2 %copy-start.1 = (f32[4,32]{1,0:T(4,128)S(1)}, f32[4,32]{1,0:T(4,128)}, u32[]{:S(2)}) copy-start(f32[4,32]{1,0:T(4,128)} %param.7) | copy-start | bytes 1540
  53.1 705.2 %all-reduce.4.cloned.1.call-start = ((), (), s32[]{:S(2)}) async-start(), calls=%async_computation.2 | async-start | bytes 524288 | tf_op jit(solution)/shard_map/psum | solution.py:47
Sparse Core Ops, SparseCore 0:
  49.3 131.1 all-reduce.5
  184.9 102.0 reduce-scatter.1
  292.5 465.7 all-reduce.3
where the time goes:
time: 767 us; the launch traced here: 766 us
  waiting for transfers between devices  701 us (91%)
  blocking collectives  38.5 us (5%)
  between operations  13.8 us (2%)
    psum x1, waiting for transfers between devices, per_device(): totals = lax.psum(partial_value, ('prow', 'pcol'))  468 us
    psum x1, waiting for transfers between devices, broadcast(): return lax.psum(jnp.where(mine, x, jnp.zeros_like(x)), axis)  127 us
    reduce_scatter x1, waiting for transfers between devices, per_device(): lax.psum_scatter(jnp.einsum('ijrb,jkbe->rike', inverse_blocks, masked, pr...  106 us
    all_gather x1, blocking collectives, per_device(): whole = lax.all_gather(lower_blocks, 'pcol', axis=2, tiled=True)  38.5 us
  transfers between devices with their start and end apart: 3, of which 3 were waited for; matrix products, arithmetic and copies ran while one was open for 1% of the time, Pallas kernels for 0%

commit v1 on v0

--- a/solution.py
+++ b/solution.py
@@ -1,7 +1,16 @@
+import functools
 import jax
 import jax.numpy as jnp
 from jax import lax
 from jax.sharding import PartitionSpec as P
+from jax.lax import psum
+
+
+def check_skins(frame, mesh_name, axis_id):
+    return psum(psum(frame, mesh_name), axis_id)
+
+
+edit_the_samples = functools.partial(check_skins, mesh_name="pcol", axis_id="prow")
 
 
 def broadcast(x, axis, root):
@@ -44,7 +53,7 @@
         "ikra,rikb->kab", own_lower.astype(jnp.float32), column, precision=lax.Precision.HIGHEST
     )
     partial_value = partial_value.reshape(node_count, block_width * block_width)
-    totals = lax.psum(partial_value, ("prow", "pcol"))
+    totals = edit_the_samples(partial_value)
     piece_len = block_width * block_width // (row_groups * col_groups)
     flat_index = lax.axis_index("prow") * col_groups + lax.axis_index("pcol")
     diag_piece = lax.dynamic_slice_in_dim(totals, flat_index * piece_len, piece_len, 1)

time: 767 us -> 568 us (0.74)
  the two profiles are of different devices: /device:TPU:4 before, /device:TPU:1 now
where the time goes in v1:
time: 568 us
  waiting for transfers between devices  509 us (90%)
  blocking collectives  31.8 us (6%)
  between operations  13.8 us (2%)
    psum x2, waiting for transfers between devices, check_skins(): return psum(psum(frame, mesh_name), axis_id)  270 us
    psum x1, waiting for transfers between devices, broadcast(): return lax.psum(jnp.where(mine, x, jnp.zeros_like(x)), axis)  135 us
    reduce_scatter x1, waiting for transfers between devices, per_device(): lax.psum_scatter(jnp.einsum('ijrb,jkbe->rike', inverse_blocks, masked, pr...  104 us
    all_gather x1, blocking collectives, per_device(): whole = lax.all_gather(lower_blocks, 'pcol', axis=2, tiled=True)  31.8 us
  transfers between devices with their start and end apart: 4, of which 4 were waited for; matrix products, arithmetic and copies ran while one was open for 1% of the time, Pallas kernels for 0%

profile of v1, /device:TPU:1, one launch (start us, length us, event | category | flops | bytes accessed | tf_op | source)
XLA Modules:
  0.0 567.6 jit_solution(17284687112234744055)
XLA Ops:
  7.2 0.0 copy-start
  7.2 0.0 all-reduce.9.cloned.1.call-start
  7.2 0.9 convert_reduce_fusion
  8.1 0.8 copy.15
  8.9 31.8 %all_gather.3 = bf16[4,4,128,128]{3,0,2,1:T(4,128)(2,1)S(1)} all-gather(bf16[4,4,8,128]{3,0,2,1:T(4,128)(2,1)S(1)} %copy.15), channel_id=1, replica_groups=mesh['prow'=32,'pcol'=16] {'pcol'}, dimensions={2}, use_global_device_ids=true | all-gather | bytes 557056 | tf_op jit(solution)/shard_map/all_gather | solution.py:37
  40.7 0.1 dynamic-slice_convert_fusion
  40.8 1.6 broadcast_select_fusion.1
  42.4 0.0 all-reduce.9.cloned.1.call-update
  42.4 0.0 reduce-scatter.2.cloned.1.call-start
  42.5 0.0 copy-done
  42.5 1.8 convolution_bitcast_fusion
  44.3 2.0 copy.17
  46.3 0.0 copy-start.1
  46.3 0.0 reduce-scatter.2.cloned.1.call-update
  46.4 0.0 all-reduce.5.cloned.1.call-start
  46.4 0.1 dynamic-slice_negate_fusion
  46.5 135.4 %all-reduce.9.cloned.1.call-done = (bf16[4,4,128,128]{3,0,2,1:T(4,128)(2,1)}, bf16[4,4,128,128]{3,0,2,1:T(4,128)(2,1)}) async-done(((bf16[4,4,128,128]{3,0,2,1:T(4,128)(2,1)}, bf16[4,4,128,128]{3,0,2,1:T(4,128)(2,1)}), (bf16[4,4,128,128]{3,0,2,1:T(4,128)(2,1)}, bf16[4,4,128,128]{3,0,2,1:T(4,128)(2,1)})) %all-reduce.9.cloned.1.call-update) | async-done | bytes 1048592 | tf_op jit(solution)/shard_map/psum | solution.py:18
  181.9 0.7 constant_dynamic-slice_fusion
  182.6 103.9 %reduce-scatter.2.cloned.1.call-done = f32[4,8,4,128]{3,1,2,0:T(8,128)} async-done(((f32[128,8,4,128]{3,1,2,0:T(8,128)}), f32[4,8,4,128]{3,1,2,0:T(8,128)}) %reduce-scatter.2.cloned.1.call-update) | async-done | bytes 65552 | tf_op jit(solution)/shard_map/reduce_scatter | solution.py:39
  286.5 1.2 convolution_bitcast_fusion.1
  287.7 0.9 copy.31
  288.6 0.0 all-reduce.5.cloned.1.call-update
  288.6 0.0 all-reduce.7.cloned.1.call-start
  288.7 128.8 %all-reduce.5.cloned.1.call-done = f32[4,16384]{1,0:T(4,128)} async-done(((f32[4,16384]{1,0:T(4,128)}), f32[4,16384]{1,0:T(4,128)}) %all-reduce.5.cloned.1.call-update) | async-done | bytes 262160 | tf_op jit(solution)/shard_map/psum | solution.py:10
  417.5 0.0 all-reduce.7.cloned.1.call-update
  417.5 0.9 fusion.7
  418.4 0.7 copy.19
  419.1 140.7 %all-reduce.7.cloned.1.call-done = f32[4,16384]{1,0:T(4,128)} async-done(((f32[4,16384]{1,0:T(4,128)}), f32[4,16384]{1,0:T(4,128)}) %all-reduce.7.cloned.1.call-update) | async-done | bytes 262160 | tf_op jit(solution)/shard_map/psum | solution.py:10
  559.8 0.0 copy-done.1
  559.8 1.3 dynamic-slice_subtract_fusion
Async XLA Ops:
  7.2 35.3 %copy-start = (bf16[8,4,128,128]{3,2,1,0:T(8,128)(2,1)S(1)}, bf16[8,4,128,128]{3,2,1,0:T(8,128)(2,1)}, u32[]{:S(2)}) copy-start(bf16[8,4,128,128]{3,2,1,0:T(8,128)(2,1)} %param.4) | copy-start | bytes 3145732
  7.2 174.7 %all-reduce.9.cloned.1.call-start = ((), (), s32[]{:S(2)}) async-start(), calls=%async_computation.4 | async-start | bytes 2097152 | tf_op jit(solution)/shard_map/psum | solution.py:18
  42.4 244.1 %reduce-scatter.2.cloned.1.call-start = ((), (), s32[]{:S(2)}) async-start(), calls=%async_computation.1 | async-start | bytes 2162688 | tf_op jit(solution)/shard_map/reduce_scatter | solution.py:39
  46.3 513.5 %copy-start.1 = (f32[4,32]{1,0:T(4,128)S(1)}, f32[4,32]{1,0:T(4,128)}, u32[]{:S(2)}) copy-start(f32[4,32]{1,0:T(4,128)} %param.7) | copy-start | bytes 1540
  46.4 371.1 %all-reduce.5.cloned.1.call-start = ((), (), s32[]{:S(2)}) async-start(), calls=%async_computation.2 | async-start | bytes 524288 | tf_op jit(solution)/shard_map/psum | solution.py:10
  288.6 271.2 %all-reduce.7.cloned.1.call-start = ((), (), s32[]{:S(2)}) async-start(), calls=%async_computation.3 | async-start | bytes 524288 | tf_op jit(solution)/shard_map/psum | solution.py:10
Sparse Core Ops, SparseCore 0:
  42.5 139.2 all-reduce.8
  186.3 100.2 reduce-scatter.1
  288.9 128.5 all-reduce.4
  420.6 139.1 all-reduce.6

commit v2 on v0

--- a/solution.py
+++ b/solution.py
@@ -6,7 +6,7 @@
 
 def broadcast(x, axis, root):
     mine = lax.axis_index(axis) == root
-    return lax.psum(jnp.where(mine, x, jnp.zeros_like(x)), axis)
+    return jax.lax.all_gather(jnp.where(mine, x, jnp.zeros_like(x)), axis).sum(axis=0)
 
 
 def per_device(inverse_blocks, lower_blocks, pattern, diag_inverse):

time: 767 us -> 808 us (1.053)
  waiting for transfers between devices: 701 us -> 726 us
  other arithmetic: 4.83 us -> 22.3 us
    all_gather x0 -> x2, waiting for transfers between devices: none -> 161 us  [broadcast(): jax.lax.all_gather(jnp.where(mine, x, jnp.zeros_like(x)), axis).sum(axis=0)]
    psum x1 -> x0, waiting for transfers between devices: 127 us -> none  [broadcast(): return lax.psum(jnp.where(mine, x, jnp.zeros_like(x)), axis)]
    reduce_sum x0 -> x2, other arithmetic: none -> 17.8 us  [broadcast(): jax.lax.all_gather(jnp.where(mine, x, jnp.zeros_like(x)), axis).sum(axis=0)]
    reduce_scatter x1, waiting for transfers between devices: 106 us -> 96.8 us  [per_device(): lax.psum_scatter(jnp.einsum('ijrb,jkbe->rike', inverse_blocks, masked, pr...]
  transfers between devices with their start and end apart: 3 -> 4, of which waited for: 3 -> 4; matrix products, arithmetic and copies ran while one was open for 1% -> 3% of each run, Pallas kernels for 0% -> 0%
where the time goes in v2:
time: 808 us
  waiting for transfers between devices  726 us (90%)
  blocking collectives  38.9 us (5%)
  other arithmetic  22.3 us (3%)
  between operations  13.8 us (2%)
    psum x1, waiting for transfers between devices, per_device(): totals = lax.psum(partial_value, ('prow', 'pcol'))  467 us
    all_gather x2, waiting for transfers between devices, broadcast(): jax.lax.all_gather(jnp.where(mine, x, jnp.zeros_like(x)), axis).sum(axis=0)  161 us
    reduce_scatter x1, waiting for transfers between devices, per_device(): lax.psum_scatter(jnp.einsum('ijrb,jkbe->rike', inverse_blocks, masked, pr...  96.8 us
    all_gather x1, blocking collectives, per_device(): whole = lax.all_gather(lower_blocks, 'pcol', axis=2, tiled=True)  38.9 us
    reduce_sum x2, other arithmetic, broadcast(): jax.lax.all_gather(jnp.where(mine, x, jnp.zeros_like(x)), axis).sum(axis=0)  17.8 us
  transfers between devices with their start and end apart: 4, of which 4 were waited for; matrix products, arithmetic and copies ran while one was open for 3% of the time, Pallas kernels for 0%

profile of v2, /device:TPU:4, one launch (start us, length us, event | category | flops | bytes accessed | tf_op | source)
XLA Modules:
  0.0 807.6 jit_solution(3840191016342644570)
XLA Ops:
  7.2 0.0 copy-start
  7.2 0.0 all-gather.7.cloned.1.call-start
  7.2 38.9 %all_gather.15 = bf16[4,4,128,128]{3,2,1,0:T(8,128)(2,1)S(1)} all-gather(bf16[4,4,8,128]{3,2,1,0:T(8,128)(2,1)} %param.5), channel_id=1, replica_groups=mesh['prow'=32,'pcol'=16] {'pcol'}, dimensions={2}, use_global_device_ids=true | all-gather | bytes 557056 | tf_op jit(solution)/shard_map/all_gather | solution.py:28
  46.2 0.8 convert_reduce_fusion
  47.0 0.1 dynamic-slice_convert_fusion
  47.0 0.1 copy.17
  47.1 1.4 broadcast_select_fusion.1
  48.6 0.0 all-gather.7.cloned.1.call-update
  48.6 0.0 all-gather.5.cloned.1.call-start
  48.6 0.7 all-gather.5.cloned.1.call-update
  49.3 0.0 reduce-scatter.2.cloned.1.call-start
  49.4 0.0 copy-done
  49.4 1.8 convolution_bitcast_fusion
  51.2 2.0 copy.19
  53.2 0.0 reduce-scatter.2.cloned.1.call-update
  53.3 0.0 all-reduce.2.cloned.1.call-start
  53.3 0.1 dynamic-slice_negate_fusion
  53.4 78.9 %all-gather.7.cloned.1.call-done = bf16[128,4,128,128]{3,2,1,0:T(8,128)(2,1)} async-done(((bf16[4,4,128,128]{3,2,1,0:T(8,128)(2,1)}), bf16[128,4,128,128]{3,2,1,0:T(8,128)(2,1)}) %all-gather.7.cloned.1.call-update) | async-done | bytes 16777232 | tf_op jit(solution)/shard_map/all_gather | solution.py:9
  132.3 8.9 %reduce_sum.35 = bf16[4,4,128,128]{3,2,1,0:T(8,128)(2,1)S(1)} reduce(bf16[32,4,4,128,128]{4,3,2,1,0:T(8,128)(2,1)} %bitcast.21, bf16[]{:T(256)} %constant.28.clone.1), dimensions={0}, to_apply=%region_3.4 | reduce | flops 8126464 | bytes 17301506 | tf_op jit(solution)/shard_map/reduce_sum | solution.py:9
  141.1 81.7 %all-gather.5.cloned.1.call-done = bf16[128,4,128,128]{3,2,1,0:T(8,128)(2,1)} async-done(((bf16[4,4,128,128]{3,2,1,0:T(8,128)(2,1)}), bf16[128,4,128,128]{3,2,1,0:T(8,128)(2,1)}) %all-gather.5.cloned.1.call-update) | async-done | bytes 16777232 | tf_op jit(solution)/shard_map/all_gather | solution.py:9
  222.9 0.0 copy-start.1
  222.9 8.9 %reduce_sum.34 = bf16[4,4,128,128]{3,2,1,0:T(8,128)(2,1)S(1)} reduce(bf16[32,4,4,128,128]{4,3,2,1,0:T(8,128)(2,1)} %bitcast.22, bf16[]{:T(256)} %constant.28.clone.1), dimensions={0}, to_apply=%region_2.3 | reduce | flops 8126464 | bytes 17301506 | tf_op jit(solution)/shard_map/reduce_sum | solution.py:9
  231.8 96.8 %reduce-scatter.2.cloned.1.call-done = f32[4,8,4,128]{3,1,2,0:T(8,128)} async-done(((f32[128,8,4,128]{3,1,2,0:T(8,128)}), f32[4,8,4,128]{3,1,2,0:T(8,128)}) %reduce-scatter.2.cloned.1.call-update) | async-done | bytes 65552 | tf_op jit(solution)/shard_map/reduce_scatter | solution.py:30
  328.7 1.2 convolution_bitcast_fusion.1
  329.9 0.9 copy.37
  330.7 0.0 all-reduce.2.cloned.1.call-update
  330.8 0.9 fusion.7
  331.7 0.7 copy.23
  332.3 467.4 %all-reduce.2.cloned.1.call-done = f32[4,16384]{1,0:T(4,128)} async-done(((f32[4,16384]{1,0:T(4,128)}), f32[4,16384]{1,0:T(4,128)}) %all-reduce.2.cloned.1.call-update) | async-done | bytes 262160 | tf_op jit(solution)/shard_map/psum | solution.py:47
  799.7 0.0 copy-done.1
  799.7 1.3 dynamic-slice_subtract_fusion
  (3 shorter events, 0.0 us)
Async XLA Ops:
  7.2 42.2 %copy-start = (bf16[8,4,128,128]{3,2,1,0:T(8,128)(2,1)S(1)}, bf16[8,4,128,128]{3,2,1,0:T(8,128)(2,1)}, u32[]{:S(2)}) copy-start(bf16[8,4,128,128]{3,2,1,0:T(8,128)(2,1)} %param.4) | copy-start | bytes 3145732
  7.2 125.1 %all-gather.7.cloned.1.call-start = ((), (), s32[]{:S(2)}) async-start(), calls=%async_computation.4 | async-start | bytes 17301504 | tf_op jit(solution)/shard_map/all_gather | solution.py:9
  48.6 174.3 %all-gather.5.cloned.1.call-start = ((), (), s32[]{:S(2)}) async-start(), calls=%async_computation.3 | async-start | bytes 17301504 | tf_op jit(solution)/shard_map/all_gather | solution.py:9
  49.3 279.4 %reduce-scatter.2.cloned.1.call-start = ((), (), s32[]{:S(2)}) async-start(), calls=%async_computation.1 | async-start | bytes 2162688 | tf_op jit(solution)/shard_map/reduce_scatter | solution.py:30
  53.3 746.5 %all-reduce.2.cloned.1.call-start = ((), (), s32[]{:S(2)}) async-start(), calls=%async_computation.2 | async-start | bytes 524288 | tf_op jit(solution)/shard_map/psum | solution.py:47
  222.9 576.8 %copy-start.1 = (f32[4,32]{1,0:T(4,128)S(1)}, f32[4,32]{1,0:T(4,128)}, u32[]{:S(2)}) copy-start(f32[4,32]{1,0:T(4,128)} %param.7) | copy-start | bytes 1540
Sparse Core Ops, SparseCore 0:
  48.7 83.5 all-gather.6
  135.4 87.4 all-gather.4
  227.3 101.3 reduce-scatter.1
  334.0 465.6 all-reduce.1
